TPU v7x, 32 devices: a whole 2x2x4 slice. The times are simulated.
32 devices in a mesh: groups: 2 (over y), blk: 8 (over z, x), heads: 2 (over core).
Axes of the slice: x: 2, y: 2, z: 4, core: 2. Of those that a mesh axis runs over, the one named last changes fastest.
Arguments:
- queries: bfloat16 [16, 64, 128], P(('groups', 'blk'), 'heads'), parts along dimension 0, may hold values from -256 to 256
- prefix_keys: bfloat16 [4096, 8, 128], P(('groups', 'blk'), 'heads'), parts along dimension 0, may hold values from -12 to 12
- prefix_values: bfloat16 [4096, 8, 128], P(('groups', 'blk'), 'heads'), parts along dimension 0, may hold values from -12 to 12
- suffix_pool: bfloat16 [48, 2, 16, 8, 128], P(('groups', 'blk'), None, None, 'heads'), parts along dimension 0, may hold values from -8.375 to 8.375
- page_owner: int32 [6, 8], P('groups'), parts along dimension 0, may hold values from 0 to 7, as said below
- page_slot: int32 [6, 8], P('groups'), parts along dimension 0, may hold values from 0 to 2, as said below
- suffix_len: int32 [6], P('groups'), parts along dimension 0, may hold values from 1 to 128, as said below
- row_request: int32 [16], P('groups'), parts along dimension 0, may hold values from 0 to 2, as said below
Outputs:
- attn_out: bfloat16 [16, 64, 128], P(('groups', 'blk'), 'heads'), parts along dimension 0
There are 2 independent parts, one for each index of `groups`. A program takes and returns all parts, laid end to end along the dimension named above; each array names one. Nothing has to cross between parts.
Inputs may be any that keep to these rules, and one draw needn't show every extreme that they name: `row_request`: rows 0 to 5 belong to one request, whose last 6 suffix tokens they are, in order; each later row is the only row of its request; every request has rows. `suffix_len`: counts the rows' own tokens; the prefill span's request has 6 or more, and some other request has exactly 128. Each request has one page on every blk index: page j lies on (page_owner[r, 0] + j) modulo the number of blk indices. `page_slot`: A local slot of the owner's pool; two requests never share a slot on one owner.
All inputs are finite; a program needn't handle non-finite values.
Results may differ from a plain program's by a relative error of at most 0.005.
Values may be sent and summed in bfloat16 or wider, within the bound.
A program may use at most 64 MiB of HBM per device.

v0:
```python
import math
import jax
import jax.numpy as jnp
from jax import lax
from jax.sharding import PartitionSpec as P


def merge_parts(first, second):
    first_max, first_sum, first_acc = first
    second_max, second_sum, second_acc = second
    highest = jnp.maximum(first_max, second_max)
    first_weight = jnp.exp(first_max - highest)
    second_weight = jnp.exp(second_max - highest)
    return (
        highest,
        first_sum * first_weight + second_sum * second_weight,
        first_acc * first_weight[..., None] + second_acc * second_weight[..., None],
    )


def prefix_part(query_rows, prefix_keys, prefix_values, kblock):
    row_count, qheads, head_dim = query_rows.shape
    kv_heads = prefix_keys.shape[1]
    group = qheads // kv_heads
    score_scale = 1.0 / math.sqrt(head_dim)
    grouped = query_rows.reshape(row_count, kv_heads, group, head_dim)
    block_total = prefix_keys.shape[0] // kblock
    key_blocks = prefix_keys.reshape(block_total, kblock, kv_heads, head_dim)
    value_blocks = prefix_values.reshape(block_total, kblock, kv_heads, head_dim)

    def key_step(running, blocks):
        run_max, run_sum, run_acc = running
        key_blk, value_blk = blocks
        scores = (
            jnp.einsum("rgqd,kgd->rgqk", grouped, key_blk, preferred_element_type=jnp.float32)
            * score_scale
        )
        new_max = jnp.maximum(run_max, jnp.max(scores, axis=-1))
        rescale = jnp.exp(run_max - new_max)
        probs = jnp.exp(scores - new_max[..., None])
        run_sum = run_sum * rescale + jnp.sum(probs, axis=-1)
        run_acc = run_acc * rescale[..., None] + jnp.einsum(
            "rgqk,kgd->rgqd",
            probs.astype(jnp.bfloat16),
            value_blk,
            preferred_element_type=jnp.float32,
        )
        return ((new_max, run_sum, run_acc), None)

    initial = (
        jnp.full((row_count, kv_heads, group), -1e30, jnp.float32),
        jnp.zeros((row_count, kv_heads, group), jnp.float32),
        jnp.zeros((row_count, kv_heads, group, head_dim), jnp.float32),
    )
    (run_max, run_sum, run_acc), _ = lax.scan(key_step, initial, (key_blocks, value_blocks))
    return (
        run_max.reshape(row_count, qheads),
        run_sum.reshape(row_count, qheads),
        run_acc.reshape(row_count, qheads, head_dim),
    )


def paged_part(query_rows, page_keys, page_values, visible):
    row_count, qheads, head_dim = query_rows.shape
    kv_heads = page_keys.shape[2]
    group = qheads // kv_heads
    score_scale = 1.0 / math.sqrt(head_dim)
    grouped = query_rows.reshape(row_count, kv_heads, group, head_dim)
    scores = (
        jnp.einsum("rgqd,rkgd->rgqk", grouped, page_keys, preferred_element_type=jnp.float32)
        * score_scale
    )
    shown = visible[:, None, None, :]
    scores = jnp.where(shown, scores, -1e30)
    highest = jnp.max(scores, axis=-1)
    probs = jnp.where(shown, jnp.exp(scores - highest[..., None]), 0.0)
    totals = jnp.sum(probs, axis=-1)
    mixed = jnp.einsum(
        "rgqk,rkgd->rgqd",
        probs.astype(jnp.bfloat16),
        page_values,
        preferred_element_type=jnp.float32,
    )
    return (
        highest.reshape(row_count, qheads),
        totals.reshape(row_count, qheads),
        mixed.reshape(row_count, qheads, head_dim),
    )


def on_device(
    queries, prefix_keys, prefix_values, suffix_pool, page_owner, page_slot, suffix_len, row_request
):
    block_count = lax.axis_size("blk")
    self_index = lax.axis_index("blk")
    rows_dev, qheads, head_dim = queries.shape
    page_len = suffix_pool.shape[2]
    row_count = row_request.shape[0]
    req_count = suffix_len.shape[0]
    kblock = min(prefix_keys.shape[0], 256)
    row_order = jnp.arange(row_count, dtype=jnp.int32)
    same_req = row_request[:, None] == row_request[None, :]
    later_rows = jnp.sum(
        (same_req & (row_order[None, :] > row_order[:, None])).astype(jnp.int32), axis=1
    )
    one_hot = (row_request[:, None] == jnp.arange(req_count, dtype=jnp.int32)[None, :]).astype(
        jnp.int32
    )
    limits = jnp.sum(one_hot * suffix_len[None, :], axis=1) - later_rows
    home_owner = jnp.sum(one_hot * page_owner[None, :, 0], axis=1)
    own_slot = jnp.sum(jnp.where(page_owner == self_index, page_slot, 0), axis=1)
    row_slot = jnp.sum(one_hot * own_slot[None, :], axis=1)
    page_index = (self_index - home_owner) % block_count
    all_rows = lax.all_gather(queries, "blk", axis=0, tiled=True)
    partial_value = prefix_part(all_rows, prefix_keys, prefix_values, kblock)
    first_token = page_index * page_len
    page_data = suffix_pool[row_slot]
    visible = (
        first_token[:, None] + jnp.arange(page_len, dtype=jnp.int32)[None, :] < limits[:, None]
    )
    partial_value = merge_parts(
        partial_value, paged_part(all_rows, page_data[:, 0], page_data[:, 1], visible)
    )
    sectioned = (
        partial_value[0].reshape(block_count, rows_dev, qheads),
        partial_value[1].reshape(block_count, rows_dev, qheads),
        partial_value[2].reshape(block_count, rows_dev, qheads, head_dim),
    )
    part_max = lax.all_to_all(sectioned[0], "blk", split_axis=0, concat_axis=0, tiled=True)
    part_sum = lax.all_to_all(sectioned[1], "blk", split_axis=0, concat_axis=0, tiled=True)
    part_acc = lax.all_to_all(sectioned[2], "blk", split_axis=0, concat_axis=0, tiled=True)
    highest = jnp.max(part_max, axis=0)
    weight = jnp.exp(part_max - highest[None])
    return (
        jnp.sum(part_acc * weight[..., None], axis=0)
        / jnp.sum(part_sum * weight, axis=0)[..., None]
    ).astype(jnp.bfloat16)


def solution(mesh):
    placed = (
        P(("groups", "blk"), "heads", None),
        P(("groups", "blk"), "heads", None),
        P(("groups", "blk"), "heads", None),
        P(("groups", "blk"), None, None, "heads", None),
        P("groups", None),
        P("groups", None),
        P("groups"),
        P("groups"),
    )
    return jax.shard_map(
        on_device,
        mesh=mesh,
        in_specs=placed,
        out_specs=P(("groups", "blk"), "heads", None),
        check_vma=False,
    )
```

profile of v0, /device:TPU:0, one launch (start us, length us, event | category | flops | bytes accessed | tf_op | source)
XLA Modules:
  0.0 72.5 jit_solution(9709522602568486579)
XLA Ops:
  0.0 0.0 copy-start
  0.0 0.0 copy-start.3
  0.0 0.7 copy-done.3
  0.7 0.0 copy-start.5
  0.7 0.0 copy-start.4
  0.7 0.1 slice_reduce_fusion
  0.8 0.5 copy-done.5
  1.4 0.2 convert_reduce_fusion
  1.6 0.0 copy-done.4
  1.6 0.0 copy-start.6
  1.6 0.1 select_reduce_fusion.1
  1.7 0.5 copy-done.6
  2.2 0.1 select_reduce_fusion.3
  2.4 1.7 %gather_fusion = bf16[8,2,16,4,128]{4,3,2,1,0:T(4,128)(2,1)S(1)} fusion(bf16[3,2,16,4,128]{4,3,2,1,0:T(4,128)(2,1)} %param.11, s32[1024]{0:T(1024)S(1)} %pad_clamp_fusion), kind=kCustom, calls=%fused_computation | custom fusion | bytes 524320 | tf_op jit(solution)/shard_map/gather | solution.py:117
  4.0 0.0 copy-start.2
  4.0 0.1 fusion.29
  4.1 0.6 copy-done.2
  4.7 32.3 %all_gather.3 = bf16[8,32,128]{2,1,0:T(8,128)(2,1)S(1)} all-gather(bf16[1,32,128]{2,1,0:T(8,128)(2,1)S(1)} %copy-done.2), channel_id=1, replica_groups=mesh['groups'=2,'blk'=8,'heads'=2] {'blk'}, dimensions={0}, use_global_device_ids=true | all-gather | bytes 73728 | tf_op jit(solution)/shard_map/all_gather | solution.py:114
  37.1 0.1 add_compare_fusion
  37.1 0.0 copy-start.1
  37.1 0.3 fusion.31
  37.4 0.1 reshape.286
  37.5 0.2 fusion.13
  37.7 0.1 reshape.287
  37.8 0.3 copy-done.1
  38.1 0.3 fusion.30
  38.4 0.2 fusion.9
  38.6 0.1 reduce_sum.97
  38.7 0.1 max.64
  38.8 0.6 multiply_add_fusion
  39.4 5.5 %all-to-all-start.1 = ((f32[8,1,32]{2,1,0:T(1,128)}), f32[8,1,32]{2,1,0:T(1,128)S(1)}, u32[]{:S(2)}, u32[]{:S(2)}) async-start(f32[8,1,32]{2,1,0:T(1,128)} %bitcast.13), calls=%async_computation.1 | async-start | bytes 8192 | tf_op jit(solution)/shard_map/all_to_all | solution.py:129
  44.9 0.1 reshape.284
  45.0 0.1 max.62
  45.0 0.0 copy-done
  45.0 0.2 fusion.1
  45.3 6.1 %all-to-all-done.1 = f32[8,1,32]{2,1,0:T(1,128)S(1)} async-done(((f32[8,1,32]{2,1,0:T(1,128)}), f32[8,1,32]{2,1,0:T(1,128)S(1)}, u32[]{:S(2)}, u32[]{:S(2)}) %all-to-all-start.1) | async-done | bytes 1056 | tf_op jit(solution)/shard_map/all_to_all | solution.py:129
  51.4 3.3 %all-to-all-start.2 = ((f32[8,1,32]{2,1,0:T(1,128)}), f32[8,1,32]{2,1,0:T(1,128)S(1)}, u32[]{:S(2)}, u32[]{:S(2)}) async-start(f32[8,1,32]{2,1,0:T(1,128)} %bitcast.16), calls=%async_computation.2 | async-start | bytes 8192 | tf_op jit(solution)/shard_map/all_to_all | solution.py:130
  54.7 0.9 %fusion.6 = f32[8,1,32,128]{3,2,1,0:T(8,128)} fusion(bf16[8,1,16,4,128]{4,3,2,1,0:T(4,128)(2,1)S(1)} %get-tuple-element.34, f32[8,4,8,128]{3,2,0,1:T(8,128)S(1)} %fusion.1, f32[8,4,8,16]{3,2,1,0:T(8,128)S(1)} %get-tuple-element.42, f32[8,32]{1,0:T(8,128)S(1)} %get-tuple-element.38, f32[8,4,8]{2,1,0:T(4,128)S(1)} %get-tuple-element.41, ...), kind=kOutput, calls=%fused_computation.11 | convolution fusion | flops 1159168 | bytes 412800 | tf_op jit(solution)/shard_map/rgqk,rkgd->rgqd/dot_general | solution.py:78
  55.6 5.5 %all-to-all-done.2 = f32[8,1,32]{2,1,0:T(1,128)S(1)} async-done(((f32[8,1,32]{2,1,0:T(1,128)}), f32[8,1,32]{2,1,0:T(1,128)S(1)}, u32[]{:S(2)}, u32[]{:S(2)}) %all-to-all-start.2) | async-done | bytes 1056 | tf_op jit(solution)/shard_map/all_to_all | solution.py:130
  61.1 3.4 %all-to-all-start = ((f32[8,1,32,128]{3,2,1,0:T(8,128)}), f32[8,1,32,128]{3,2,1,0:T(8,128)S(1)}, u32[]{:S(2)}, u32[]{:S(2)}) async-start(f32[8,1,32,128]{3,2,1,0:T(8,128)} %fusion.6), calls=%async_computation | async-start | bytes 262144 | tf_op jit(solution)/shard_map/all_to_all | solution.py:131
  64.5 7.2 %all-to-all-done = f32[8,1,32,128]{3,2,1,0:T(8,128)S(1)} async-done(((f32[8,1,32,128]{3,2,1,0:T(8,128)}), f32[8,1,32,128]{3,2,1,0:T(8,128)S(1)}, u32[]{:S(2)}, u32[]{:S(2)}) %all-to-all-start) | async-done | bytes 131104 | tf_op jit(solution)/shard_map/all_to_all | solution.py:131
  71.7 0.1 multiply_reduce_fusion
  71.8 0.7 fusion.20
  (10 shorter events, 0.1 us)
Async XLA Ops:
  0.0 45.0 %copy-start = (bf16[256,4,128]{2,1,0:T(4,128)(2,1)S(1)}, bf16[256,4,128]{2,1,0:T(4,128)(2,1)}, u32[]{:S(2)}) copy-start(bf16[256,4,128]{2,1,0:T(4,128)(2,1)} %param.10) | copy-start | bytes 786436
  0.0 0.7 %copy-start.3 = (s32[3,8]{1,0:T(4,128)S(1)}, s32[3,8]{1,0:T(4,128)}, u32[]{:S(2)}) copy-start(s32[3,8]{1,0:T(4,128)} %param.12) | copy-start | bytes 292
  0.7 0.7 copy-start.5
  0.7 0.8 %copy-start.4 = (s32[3,8]{1,0:T(4,128)S(1)}, s32[3,8]{1,0:T(4,128)}, u32[]{:S(2)}) copy-start(s32[3,8]{1,0:T(4,128)} %param.13) | copy-start | bytes 292
  1.6 0.7 copy-start.6
  4.0 0.7 copy-start.2
  37.1 1.0 %copy-start.1 = (bf16[256,4,128]{2,1,0:T(4,128)(2,1)S(1)}, bf16[256,4,128]{2,1,0:T(4,128)(2,1)}, u32[]{:S(2)}) copy-start(bf16[256,4,128]{2,1,0:T(4,128)(2,1)} %param.9) | copy-start | bytes 786436
  39.4 12.0 %all-to-all-start.1 = ((f32[8,1,32]{2,1,0:T(1,128)}), f32[8,1,32]{2,1,0:T(1,128)S(1)}, u32[]{:S(2)}, u32[]{:S(2)}) async-start(f32[8,1,32]{2,1,0:T(1,128)} %bitcast.13), calls=%async_computation.1 | async-start | bytes 8192 | tf_op jit(solution)/shard_map/all_to_all | solution.py:129
  51.4 9.7 %all-to-all-start.2 = ((f32[8,1,32]{2,1,0:T(1,128)}), f32[8,1,32]{2,1,0:T(1,128)S(1)}, u32[]{:S(2)}, u32[]{:S(2)}) async-start(f32[8,1,32]{2,1,0:T(1,128)} %bitcast.16), calls=%async_computation.2 | async-start | bytes 8192 | tf_op jit(solution)/shard_map/all_to_all | solution.py:130
  61.1 10.7 %all-to-all-start = ((f32[8,1,32,128]{3,2,1,0:T(8,128)}), f32[8,1,32,128]{3,2,1,0:T(8,128)S(1)}, u32[]{:S(2)}, u32[]{:S(2)}) async-start(f32[8,1,32,128]{3,2,1,0:T(8,128)} %fusion.6), calls=%async_computation | async-start | bytes 262144 | tf_op jit(solution)/shard_map/all_to_all | solution.py:131
where the time goes:
time: 73 us; the launch traced here: 72.5 us
  blocking collectives  32.3 us (44%)
  waiting for transfers between devices  18.8 us (26%)
  starting transfers between devices  12.1 us (17%)
  local copies, waits for them, and re-layouts  5.05 us (7%)
  other arithmetic  2.39 us (3%)
  matrix products  1.66 us (2%)
    all_gather x1, blocking collectives, on_device(): all_rows = lax.all_gather(queries, 'blk', axis=0, tiled=True)  32.3 us
    all_to_all x1, waiting for transfers between devices, on_device(): lax.all_to_all(sectioned[2], 'blk', split_axis=0, concat_axis=0, tiled=True)  7.22 us
    all_to_all x1, waiting for transfers between devices, on_device(): lax.all_to_all(sectioned[0], 'blk', split_axis=0, concat_axis=0, tiled=True)  6.07 us
    all_to_all x1, waiting for transfers between devices, on_device(): lax.all_to_all(sectioned[1], 'blk', split_axis=0, concat_axis=0, tiled=True)  5.5 us
    all_to_all x1, starting transfers between devices, on_device(): lax.all_to_all(sectioned[0], 'blk', split_axis=0, concat_axis=0, tiled=True)  5.46 us
    all_to_all x1, starting transfers between devices, on_device(): lax.all_to_all(sectioned[2], 'blk', split_axis=0, concat_axis=0, tiled=True)  3.37 us
    all_to_all x1, starting transfers between devices, on_device(): lax.all_to_all(sectioned[1], 'blk', split_axis=0, concat_axis=0, tiled=True)  3.31 us
    unnamed x14, local copies, waits for them, and re-layouts  2.68 us
  transfers between devices with their start and end apart: 3, of which 3 were waited for; matrix products, arithmetic and copies ran while one was open for 2% of the time, Pallas kernels for 0%

commit v1 on v0

--- a/solution.py
+++ b/solution.py
@@ -3,6 +3,27 @@
 import jax.numpy as jnp
 from jax import lax
 from jax.sharding import PartitionSpec as P
+
+
+def gather_around(x, axis, dim):
+    peers, mine, width = (lax.axis_size(axis), lax.axis_index(axis), x.shape[dim])
+    ahead = [(i, (i + 1) % peers) for i in range(peers)]
+    behind = [(i, (i - 1) % peers) for i in range(peers)]
+    out = jnp.zeros((*x.shape[:dim], peers * width, *x.shape[dim + 1 :]), x.dtype)
+    out = lax.dynamic_update_slice_in_dim(out, x, mine * width, axis=dim)
+    from_left = from_right = x
+    half = peers // 2
+    for step in range(1, half + 1):
+        from_left = lax.ppermute(from_left, axis, ahead)
+        out = lax.dynamic_update_slice_in_dim(
+            out, from_left, (mine - step) % peers * width, axis=dim
+        )
+        if step < peers - half:
+            from_right = lax.ppermute(from_right, axis, behind)
+            out = lax.dynamic_update_slice_in_dim(
+                out, from_right, (mine + step) % peers * width, axis=dim
+            )
+    return out
 
 
 def merge_parts(first, second):
@@ -111,7 +132,7 @@
     own_slot = jnp.sum(jnp.where(page_owner == self_index, page_slot, 0), axis=1)
     row_slot = jnp.sum(one_hot * own_slot[None, :], axis=1)
     page_index = (self_index - home_owner) % block_count
-    all_rows = lax.all_gather(queries, "blk", axis=0, tiled=True)
+    all_rows = gather_around(queries, "blk", 0)
     partial_value = prefix_part(all_rows, prefix_keys, prefix_values, kblock)
     first_token = page_index * page_len
     page_data = suffix_pool[row_slot]

time: 73 us -> 68.1 us (0.933)
  blocking collectives: 32.3 us -> 0 us
  waiting for transfers between devices: 18.8 us -> 32.8 us
  starting transfers between devices: 12.1 us -> 25.7 us
    all_gather x1 -> x0, blocking collectives: 32.3 us -> none  [on_device(): all_rows = lax.all_gather(queries, 'blk', axis=0, tiled=True)]
    ppermute x0 -> x7, starting transfers between devices: none -> 15.7 us  [the longest x3 15.7 us: gather_around(): from_right = lax.ppermute(from_right, axis, behind)]
    ppermute x0 -> x7, waiting for transfers between devices: none -> 14 us  [the longest x4 12.6 us: gather_around(): from_left = lax.ppermute(from_left, axis, ahead)]
    all_to_all x1, starting transfers between devices: 5.46 us -> 3.33 us  [on_device(): lax.all_to_all(sectioned[0], 'blk', split_axis=0, concat_axis=0, tiled=True)]
  transfers between devices with their start and end apart: 3 -> 10, of which waited for: 3 -> 6; matrix products, arithmetic and copies ran while one was open for 2% -> 5% of each run, Pallas kernels for 0% -> 0%
where the time goes in v1:
time: 68.1 us; the launch traced here: 67.6 us
  waiting for transfers between devices  32.8 us (48%)
  starting transfers between devices  25.7 us (38%)
  local copies, waits for them, and re-layouts  4.84 us (7%)
  other arithmetic  2.39 us (4%)
  matrix products  1.66 us (2%)
    ppermute x3, starting transfers between devices, gather_around(): from_right = lax.ppermute(from_right, axis, behind)  15.7 us
    ppermute x4, waiting for transfers between devices, gather_around(): from_left = lax.ppermute(from_left, axis, ahead)  12.6 us
    all_to_all x1, waiting for transfers between devices, on_device(): lax.all_to_all(sectioned[2], 'blk', split_axis=0, concat_axis=0, tiled=True)  7.22 us
    all_to_all x1, waiting for transfers between devices, on_device(): lax.all_to_all(sectioned[0], 'blk', split_axis=0, concat_axis=0, tiled=True)  6.16 us
    all_to_all x1, waiting for transfers between devices, on_device(): lax.all_to_all(sectioned[1], 'blk', split_axis=0, concat_axis=0, tiled=True)  5.48 us
    all_to_all x1, starting transfers between devices, on_device(): lax.all_to_all(sectioned[2], 'blk', split_axis=0, concat_axis=0, tiled=True)  3.37 us
    all_to_all x1, starting transfers between devices, on_device(): lax.all_to_all(sectioned[0], 'blk', split_axis=0, concat_axis=0, tiled=True)  3.33 us
    all_to_all x1, starting transfers between devices, on_device(): lax.all_to_all(sectioned[1], 'blk', split_axis=0, concat_axis=0, tiled=True)  3.31 us
  transfers between devices with their start and end apart: 10, of which 6 were waited for; matrix products, arithmetic and copies ran while one was open for 5% of the time, Pallas kernels for 0%

profile of v1, /device:TPU:0, one launch (start us, length us, event | category | flops | bytes accessed | tf_op | source)
XLA Modules:
  0.0 67.6 jit_solution(10819442398684992052)
XLA Ops:
  0.0 0.0 copy-start
  0.0 6.0 %collective-permute-start.1 = (bf16[1,32,128]{2,1,0:T(8,128)(2,1)}, bf16[1,32,128]{2,1,0:T(8,128)(2,1)S(1)}, u32[]{:S(2)}, u32[]{:S(2)}) collective-permute-start(bf16[1,32,128]{2,1,0:T(8,128)(2,1)} %param.8), channel_id=1, source_target_pairs={{0,14},{2,0},{4,2},{6,4},{8,6},{10,8},{12,10},{14,12},{1,15},{3,1}... | collective-permute-start | bytes 24584 | tf_op jit(solution)/shard_map/ppermute | solution.py:22
  6.0 0.0 collective-permute-start
  6.0 0.7 %copy-done.2 = s32[3,8]{1,0:T(4,128)S(1)} copy-done((s32[3,8]{1,0:T(4,128)S(1)}, s32[3,8]{1,0:T(4,128)}, u32[]{:S(2)}) %copy-start.2) | copy-done | bytes 120
  6.7 0.1 slice_reduce_fusion
  6.8 0.0 copy-start.5
  6.8 0.1 select_reduce_fusion.1
  6.9 0.5 copy-done.5
  7.5 0.2 convert_reduce_fusion
  7.7 0.5 copy-done.6
  8.1 0.1 select_reduce_fusion.3
  8.3 1.7 %gather_fusion = bf16[8,2,16,4,128]{4,3,2,1,0:T(4,128)(2,1)S(1)} fusion(bf16[3,2,16,4,128]{4,3,2,1,0:T(4,128)(2,1)} %param.11, s32[1024]{0:T(1024)S(1)} %pad_clamp_fusion), kind=kCustom, calls=%fused_computation | custom fusion | bytes 524320 | tf_op jit(solution)/shard_map/gather | solution.py:138
  9.9 0.1 fusion.28
  10.0 0.1 add_compare_fusion
  10.1 0.7 %copy-done.3 = bf16[1,32,128]{2,1,0:T(8,128)(2,1)S(1)} copy-done((bf16[1,32,128]{2,1,0:T(8,128)(2,1)S(1)}, bf16[1,32,128]{2,1,0:T(8,128)(2,1)}, u32[]{:S(2)}) %copy-start.3) | copy-done | bytes 8216
  10.8 0.0 collective-permute-done.1
  10.8 4.7 %collective-permute-start.3 = (bf16[1,32,128]{2,1,0:T(8,128)(2,1)S(1)}, bf16[1,32,128]{2,1,0:T(8,128)(2,1)S(1)}, u32[]{:S(2)}, u32[]{:S(2)}) collective-permute-start(bf16[1,32,128]{2,1,0:T(8,128)(2,1)S(1)} %collective-permute-done.1), channel_id=1, source_target_pairs={{0,14},{2,0},{4,2},{6,4},{8,6},{10,8},{12,10},{14,12},{1,15},{3,1}... | collective-permute-start | bytes 24584 | tf_op jit(solution)/shard_map/ppermute | solution.py:22
  15.6 0.0 collective-permute-done
  15.6 0.0 collective-permute-start.2
  15.6 1.3 %collective-permute-done.3 = bf16[1,32,128]{2,1,0:T(8,128)(2,1)S(1)} collective-permute-done((bf16[1,32,128]{2,1,0:T(8,128)(2,1)S(1)}, bf16[1,32,128]{2,1,0:T(8,128)(2,1)S(1)}, u32[]{:S(2)}, u32[]{:S(2)}) %collective-permute-start.3) | collective-permute-done | bytes 8224 | tf_op jit(solution)/shard_map/ppermute | solution.py:22
  16.9 5.0 %collective-permute-start.5 = (bf16[1,32,128]{2,1,0:T(8,128)(2,1)S(1)}, bf16[1,32,128]{2,1,0:T(8,128)(2,1)S(1)}, u32[]{:S(2)}, u32[]{:S(2)}) collective-permute-start(bf16[1,32,128]{2,1,0:T(8,128)(2,1)S(1)} %collective-permute-done.3), channel_id=1, source_target_pairs={{0,14},{2,0},{4,2},{6,4},{8,6},{10,8},{12,10},{14,12},{1,15},{3,1}... | collective-permute-start | bytes 24584 | tf_op jit(solution)/shard_map/ppermute | solution.py:22
  21.9 0.0 collective-permute-done.2
  21.9 0.0 collective-permute-start.4
  21.9 6.3 %collective-permute-done.4 = bf16[1,32,128]{2,1,0:T(8,128)(2,1)S(1)} collective-permute-done((bf16[1,32,128]{2,1,0:T(8,128)(2,1)S(1)}, bf16[1,32,128]{2,1,0:T(8,128)(2,1)S(1)}, u32[]{:S(2)}, u32[]{:S(2)}) %collective-permute-start.4) | collective-permute-done | bytes 8224 | tf_op jit(solution)/shard_map/ppermute | solution.py:17
  28.3 0.0 collective-permute-start.6
  28.3 0.0 collective-permute-done.5
  28.3 6.3 %collective-permute-done.6 = bf16[1,32,128]{2,1,0:T(8,128)(2,1)S(1)} collective-permute-done((bf16[1,32,128]{2,1,0:T(8,128)(2,1)S(1)}, bf16[1,32,128]{2,1,0:T(8,128)(2,1)S(1)}, u32[]{:S(2)}, u32[]{:S(2)}) %collective-permute-start.6) | collective-permute-done | bytes 8224 | tf_op jit(solution)/shard_map/ppermute | solution.py:17
  34.6 0.3 fusion.30
  34.9 0.1 reshape.286
  35.0 0.1 reshape.284
  35.0 0.3 fusion.29
  35.4 0.1 max.64
  35.4 0.1 max.62
  35.5 0.2 fusion.12
  35.8 0.1 reshape.287
  35.8 0.2 fusion.8
  36.1 0.1 reduce_sum.97
  36.1 0.6 multiply_add_fusion
  36.8 3.3 %all-to-all-start.1 = ((f32[8,1,32]{2,1,0:T(1,128)}), f32[8,1,32]{2,1,0:T(1,128)S(1)}, u32[]{:S(2)}, u32[]{:S(2)}) async-start(f32[8,1,32]{2,1,0:T(1,128)} %bitcast.12), calls=%async_computation.1 | async-start | bytes 8192 | tf_op jit(solution)/shard_map/all_to_all | solution.py:150
  40.1 0.2 fusion.1
  40.4 6.2 %all-to-all-done.1 = f32[8,1,32]{2,1,0:T(1,128)S(1)} async-done(((f32[8,1,32]{2,1,0:T(1,128)}), f32[8,1,32]{2,1,0:T(1,128)S(1)}, u32[]{:S(2)}, u32[]{:S(2)}) %all-to-all-start.1) | async-done | bytes 1056 | tf_op jit(solution)/shard_map/all_to_all | solution.py:150
  46.5 3.3 %all-to-all-start.2 = ((f32[8,1,32]{2,1,0:T(1,128)}), f32[8,1,32]{2,1,0:T(1,128)S(1)}, u32[]{:S(2)}, u32[]{:S(2)}) async-start(f32[8,1,32]{2,1,0:T(1,128)} %bitcast.15), calls=%async_computation.2 | async-start | bytes 8192 | tf_op jit(solution)/shard_map/all_to_all | solution.py:151
  49.8 0.9 %fusion.5 = f32[8,1,32,128]{3,2,1,0:T(8,128)} fusion(bf16[8,1,16,4,128]{4,3,2,1,0:T(4,128)(2,1)S(1)} %get-tuple-element.34, f32[8,4,8,128]{3,2,0,1:T(8,128)S(1)} %fusion.1, f32[8,4,8,16]{3,2,1,0:T(8,128)S(1)} %get-tuple-element.42, f32[8,32]{1,0:T(8,128)S(1)} %get-tuple-element.38, f32[8,4,8]{2,1,0:T(4,128)S(1)} %get-tuple-element.41, ...), kind=kOutput, calls=%fused_computation.10 | convolution fusion | flops 1159168 | bytes 412800 | tf_op jit(solution)/shard_map/rgqk,rkgd->rgqd/dot_general | solution.py:99
  50.7 5.5 %all-to-all-done.2 = f32[8,1,32]{2,1,0:T(1,128)S(1)} async-done(((f32[8,1,32]{2,1,0:T(1,128)}), f32[8,1,32]{2,1,0:T(1,128)S(1)}, u32[]{:S(2)}, u32[]{:S(2)}) %all-to-all-start.2) | async-done | bytes 1056 | tf_op jit(solution)/shard_map/all_to_all | solution.py:151
  56.2 3.4 %all-to-all-start = ((f32[8,1,32,128]{3,2,1,0:T(8,128)}), f32[8,1,32,128]{3,2,1,0:T(8,128)S(1)}, u32[]{:S(2)}, u32[]{:S(2)}) async-start(f32[8,1,32,128]{3,2,1,0:T(8,128)} %fusion.5), calls=%async_computation | async-start | bytes 262144 | tf_op jit(solution)/shard_map/all_to_all | solution.py:152
  59.6 7.2 %all-to-all-done = f32[8,1,32,128]{3,2,1,0:T(8,128)S(1)} async-done(((f32[8,1,32,128]{3,2,1,0:T(8,128)}), f32[8,1,32,128]{3,2,1,0:T(8,128)S(1)}, u32[]{:S(2)}, u32[]{:S(2)}) %all-to-all-start) | async-done | bytes 131104 | tf_op jit(solution)/shard_map/all_to_all | solution.py:152
  66.9 0.1 multiply_reduce_fusion
  67.0 0.7 %fusion.19 = bf16[1,32,128]{2,1,0:T(8,128)(2,1)} fusion(f32[32,128]{1,0:T(8,128)S(1)} %multiply_reduce_fusion, f32[32]{0:T(128)S(1)} %get-tuple-element.20), kind=kLoop, calls=%fused_computation.29 | loop fusion | flops 8192 | bytes 24704 | tf_op jit(solution)/shard_map/convert_element_type | solution.py:158
  (27 shorter events, 0.2 us)
Async XLA Ops:
  0.0 35.0 %copy-start = (bf16[256,4,128]{2,1,0:T(4,128)(2,1)S(1)}, bf16[256,4,128]{2,1,0:T(4,128)(2,1)}, u32[]{:S(2)}) copy-start(bf16[256,4,128]{2,1,0:T(4,128)(2,1)} %param.9) | copy-start | bytes 786436
  0.0 10.8 %collective-permute-start.1 = (bf16[1,32,128]{2,1,0:T(8,128)(2,1)}, bf16[1,32,128]{2,1,0:T(8,128)(2,1)S(1)}, u32[]{:S(2)}, u32[]{:S(2)}) collective-permute-start(bf16[1,32,128]{2,1,0:T(8,128)(2,1)} %param.8), channel_id=1, source_target_pairs={{0,14},{2,0},{4,2},{6,4},{8,6},{10,8},{12,10},{14,12},{1,15},{3,1}... | collective-permute-start | bytes 24584 | tf_op jit(solution)/shard_map/ppermute | solution.py:22
  6.0 9.5 %collective-permute-start = (bf16[1,32,128]{2,1,0:T(8,128)(2,1)}, bf16[1,32,128]{2,1,0:T(8,128)(2,1)S(1)}, u32[]{:S(2)}, u32[]{:S(2)}) collective-permute-start(bf16[1,32,128]{2,1,0:T(8,128)(2,1)} %param.8), channel_id=1, source_target_pairs={{0,2},{2,4},{4,6},{6,8},{8,10},{10,12},{12,14},{14,0},{1,3},{3,5},... | collective-permute-start | bytes 24584 | tf_op jit(solution)/shard_map/ppermute | solution.py:17
  6.0 0.7 %copy-start.2 = (s32[3,8]{1,0:T(4,128)S(1)}, s32[3,8]{1,0:T(4,128)}, u32[]{:S(2)}) copy-start(s32[3,8]{1,0:T(4,128)} %param.12) | copy-start | bytes 292
  6.0 0.8 %copy-start.4 = (s32[3,8]{1,0:T(4,128)S(1)}, s32[3,8]{1,0:T(4,128)}, u32[]{:S(2)}) copy-start(s32[3,8]{1,0:T(4,128)} %param.13) | copy-start | bytes 292
  6.8 0.7 copy-start.5
  7.5 0.7 copy-start.6
  10.1 0.7 %copy-start.3 = (bf16[1,32,128]{2,1,0:T(8,128)(2,1)S(1)}, bf16[1,32,128]{2,1,0:T(8,128)(2,1)}, u32[]{:S(2)}) copy-start(bf16[1,32,128]{2,1,0:T(8,128)(2,1)} %param.8) | copy-start | bytes 24580
  10.8 6.1 %collective-permute-start.3 = (bf16[1,32,128]{2,1,0:T(8,128)(2,1)S(1)}, bf16[1,32,128]{2,1,0:T(8,128)(2,1)S(1)}, u32[]{:S(2)}, u32[]{:S(2)}) collective-permute-start(bf16[1,32,128]{2,1,0:T(8,128)(2,1)S(1)} %collective-permute-done.1), channel_id=1, source_target_pairs={{0,14},{2,0},{4,2},{6,4},{8,6},{10,8},{12,10},{14,12},{1,15},{3,1}... | collective-permute-start | bytes 24584 | tf_op jit(solution)/shard_map/ppermute | solution.py:22
  15.6 6.3 %collective-permute-start.2 = (bf16[1,32,128]{2,1,0:T(8,128)(2,1)S(1)}, bf16[1,32,128]{2,1,0:T(8,128)(2,1)S(1)}, u32[]{:S(2)}, u32[]{:S(2)}) collective-permute-start(bf16[1,32,128]{2,1,0:T(8,128)(2,1)S(1)} %collective-permute-done), channel_id=1, source_target_pairs={{0,2},{2,4},{4,6},{6,8},{8,10},{10,12},{12,14},{14,0},{1,3},{3,5},... | collective-permute-start | bytes 24584 | tf_op jit(solution)/shard_map/ppermute | solution.py:17
  16.9 11.3 %collective-permute-start.5 = (bf16[1,32,128]{2,1,0:T(8,128)(2,1)S(1)}, bf16[1,32,128]{2,1,0:T(8,128)(2,1)S(1)}, u32[]{:S(2)}, u32[]{:S(2)}) collective-permute-start(bf16[1,32,128]{2,1,0:T(8,128)(2,1)S(1)} %collective-permute-done.3), channel_id=1, source_target_pairs={{0,14},{2,0},{4,2},{6,4},{8,6},{10,8},{12,10},{14,12},{1,15},{3,1}... | collective-permute-start | bytes 24584 | tf_op jit(solution)/shard_map/ppermute | solution.py:22
  21.9 6.3 %collective-permute-start.4 = (bf16[1,32,128]{2,1,0:T(8,128)(2,1)S(1)}, bf16[1,32,128]{2,1,0:T(8,128)(2,1)S(1)}, u32[]{:S(2)}, u32[]{:S(2)}) collective-permute-start(bf16[1,32,128]{2,1,0:T(8,128)(2,1)S(1)} %collective-permute-done.2), channel_id=1, source_target_pairs={{0,2},{2,4},{4,6},{6,8},{8,10},{10,12},{12,14},{14,0},{1,3},{3,5},... | collective-permute-start | bytes 24584 | tf_op jit(solution)/shard_map/ppermute | solution.py:17
  28.3 6.3 %collective-permute-start.6 = (bf16[1,32,128]{2,1,0:T(8,128)(2,1)S(1)}, bf16[1,32,128]{2,1,0:T(8,128)(2,1)S(1)}, u32[]{:S(2)}, u32[]{:S(2)}) collective-permute-start(bf16[1,32,128]{2,1,0:T(8,128)(2,1)S(1)} %collective-permute-done.4), channel_id=1, source_target_pairs={{0,2},{2,4},{4,6},{6,8},{8,10},{10,12},{12,14},{14,0},{1,3},{3,5},... | collective-permute-start | bytes 24584 | tf_op jit(solution)/shard_map/ppermute | solution.py:17
  35.5 4.6 %copy-start.1 = (bf16[256,4,128]{2,1,0:T(4,128)(2,1)S(1)}, bf16[256,4,128]{2,1,0:T(4,128)(2,1)}, u32[]{:S(2)}) copy-start(bf16[256,4,128]{2,1,0:T(4,128)(2,1)} %param.10) | copy-start | bytes 786436
  36.8 9.8 %all-to-all-start.1 = ((f32[8,1,32]{2,1,0:T(1,128)}), f32[8,1,32]{2,1,0:T(1,128)S(1)}, u32[]{:S(2)}, u32[]{:S(2)}) async-start(f32[8,1,32]{2,1,0:T(1,128)} %bitcast.12), calls=%async_computation.1 | async-start | bytes 8192 | tf_op jit(solution)/shard_map/all_to_all | solution.py:150
  46.5 9.7 %all-to-all-start.2 = ((f32[8,1,32]{2,1,0:T(1,128)}), f32[8,1,32]{2,1,0:T(1,128)S(1)}, u32[]{:S(2)}, u32[]{:S(2)}) async-start(f32[8,1,32]{2,1,0:T(1,128)} %bitcast.15), calls=%async_computation.2 | async-start | bytes 8192 | tf_op jit(solution)/shard_map/all_to_all | solution.py:151
  56.2 10.7 %all-to-all-start = ((f32[8,1,32,128]{3,2,1,0:T(8,128)}), f32[8,1,32,128]{3,2,1,0:T(8,128)S(1)}, u32[]{:S(2)}, u32[]{:S(2)}) async-start(f32[8,1,32,128]{3,2,1,0:T(8,128)} %fusion.5), calls=%async_computation | async-start | bytes 262144 | tf_op jit(solution)/shard_map/all_to_all | solution.py:152
